TPU v7x, 32 devices: a whole 2x2x4 slice. The times are simulated.
32 devices in a mesh: slab: 32 (over z, y, x, core).
Axes of the slice: x: 2, y: 2, z: 4, core: 2. Of those that a mesh axis runs over, the one named last changes fastest.
Arguments:
- tensor: float32 [128, 1024, 512], P('slab'), may hold values from 0 to 1024
- first: float32 [128, 512], P('slab'), may hold values from 0.01 to 2.01
- second: float32 [1024, 512], replicated, may hold values from 0.01 to 2.01
- third: float32 [512, 512], replicated, may hold values from 0.01 to 2.01
Outputs:
- new_first: float32 [128, 512], P('slab')
- new_second: float32 [1024, 512], P('slab')
- new_third: float32 [512, 512], P('slab')
All inputs are finite; a program needn't handle non-finite values.
Results may differ from a plain program's by a relative error of at most 0.0002.
Values sent between devices are 32-bit elements; how exact they have to be, the bound alone decides.
No kernel may reach another device: no remote copies, remote signals or barrier semaphores. Data moves between devices by JAX's collectives and lax.ppermute only.
A program may use at most 64 MiB of HBM per device.

v0:
```python
import jax
import jax.numpy as jnp
from jax import lax
from jax.sharding import PartitionSpec as P


def update(start_rows, sums, gram):
    highest = lax.Precision.HIGHEST
    lipschitz = jnp.max(jnp.sum(gram, axis=1))
    previous = start_rows
    extrapolated = start_rows
    updated = start_rows
    for turn in range(4):
        gradient = jnp.dot(extrapolated, gram, precision=highest) - sums
        updated = jnp.maximum(extrapolated - gradient / lipschitz, 0.0)
        extrapolated = updated + turn / (turn + 3.0) * (updated - previous)
        previous = updated
    return updated


def body(tensor, first, second, third):
    highest = lax.Precision.HIGHEST
    devices_count = lax.axis_size("slab")
    device_index = lax.axis_index("slab")
    second_count = second.shape[0] // devices_count
    third_count = third.shape[0] // devices_count
    gram_second = jnp.dot(second.T, second, precision=highest)
    gram_third = jnp.dot(third.T, third, precision=highest)
    partial_value = jnp.einsum("ijk,kr->ijr", tensor, third, precision=highest)
    first_sums = jnp.einsum("ijr,jr->ir", partial_value, second, precision=highest)
    new_first = update(first, first_sums, gram_second * gram_third)
    own_gram = jnp.dot(new_first.T, new_first, precision=highest)
    gram_first = lax.psum(own_gram, "slab")
    own_term = jnp.einsum("ijr,ir->jr", partial_value, new_first, precision=highest)
    second_sums = lax.psum(own_term, "slab")
    whole_second = update(second, second_sums, gram_first * gram_third)
    weighted = whole_second[None, :, :] * new_first[:, None, :]
    third_sums = jnp.einsum("ijk,ijr->kr", tensor, weighted, precision=highest)
    gram_new_second = jnp.dot(whole_second.T, whole_second, precision=highest)
    out_second = lax.dynamic_slice_in_dim(
        whole_second, device_index * second_count, second_count, 0
    )
    third_rows = lax.psum_scatter(third_sums, "slab", scatter_dimension=0, tiled=True)
    own_third = lax.dynamic_slice_in_dim(third, device_index * third_count, third_count, 0)
    new_third = update(own_third, third_rows, gram_first * gram_new_second)
    return (new_first, out_second, new_third)


def solution(mesh):
    in_specs = (P("slab", None, None), P("slab", None), P(), P())
    out_specs = (P("slab", None), P("slab", None), P("slab", None))
    return jax.shard_map(body, mesh=mesh, in_specs=in_specs, out_specs=out_specs, check_vma=False)
```

profile of v0, /device:TPU:0, one launch (start us, length us, event | category | flops | bytes accessed | tf_op | source)
XLA Modules:
  0.0 380.0 jit_solution(14814584285607130259)
XLA Ops:
  7.2 0.0 all-reduce.3.cloned.1.call-start
  7.2 3.5 fusion.82
  10.8 3.6 fusion.80
  14.4 0.6 reduce_max.27
  15.0 16.6 %multiply_reduce_fusion.1 = (f32[512,4]{0,1:T(4,128)S(1)}, f32[4,1024,512]{2,1,0:T(8,128)S(1)}) fusion(f32[512,1024]{0,1:T(8,128)S(1)} %bitcast.64, f32[4,1024,512]{2,1,0:T(8,128)} %param.4, f32[512,512]{1,0:T(8,128)} %param.7), kind=kOutput, calls=%fused_computation.1 | convolution fusion | flops 12889094144 | bytes 19931136 | tf_op jit(solution)/shard_map/ijk,kr->ijr/dot_general | solution.py:29
  31.7 1.6 fusion.35
  33.3 1.6 fusion.31
  34.9 1.6 fusion.28
  36.5 1.6 fusion.25
  38.2 2.1 fusion.83
  40.3 2.5 multiply_reduce_fusion
  42.8 2.9 copy.28
  45.7 0.0 reduce-scatter.2.cloned.1.call-start
  45.8 1.9 copy.8
  47.6 139.1 %all-reduce.3.cloned.1.call-done = (f32[1024,512]{0,1:T(8,128)}, f32[512,512]{0,1:T(8,128)}) async-done(((f32[1024,512]{0,1:T(8,128)}, f32[512,512]{0,1:T(8,128)}), (f32[1024,512]{0,1:T(8,128)}, f32[512,512]{0,1:T(8,128)})) %all-reduce.3.cloned.1.call-update) | async-done | bytes 3145744 | tf_op jit(solution)/shard_map/psum | solution.py:35
  186.7 2.4 fusion.79
  189.1 0.6 reduce_max.28
  189.7 8.0 %fusion.6 = f32[1024,512]{0,1:T(8,128)S(1)} fusion(f32[1024,512]{0,1:T(8,128)} %copy.8, f32[1024,512]{0,1:T(8,128)} %get-tuple-element.6, f32[512,512]{0,1:T(8,128)} %get-tuple-element.9, f32[1024,512]{1,0:T(8,128)S(1)} %copy-done, f32[]{:T(128)} %reduce_max.28), kind=kOutput, calls=%fused_computation.9 | convolution fusion | flops 3223322624 | bytes 9437188 | tf_op jit(solution)/shard_map/dot_general | solution.py:14
  197.7 3.7 fusion.40
  201.5 6.0 %multiply_add_fusion = f32[1024,512]{0,1:T(8,128)S(1)} fusion(f32[1024,512]{0,1:T(8,128)S(1)} %copy-done.8, f32[1024,512]{0,1:T(8,128)S(1)} %fusion.6, f32[512,512]{0,1:T(8,128)S(1)} %copy-done.4, f32[1024,512]{0,1:T(8,128)S(1)} %fusion.40, f32[1024,512]{0,1:T(8,128)S(1)} %copy-done.3, f32[]{:T(128)} %reduce_max.28), kind=kOutput, calls=%fused_computation.11 | convolution fusion | flops 3235381248 | bytes 11534340 | tf_op jit(solution)/shard_map/dot_general | solution.py:14
  207.5 4.6 %subtract_maximum_fusion = f32[1024,512]{0,1:T(8,128)S(1)} fusion(f32[1024,512]{0,1:T(8,128)S(1)} %multiply_add_fusion, f32[1024,512]{0,1:T(8,128)S(1)} %copy-done.8, f32[512,512]{0,1:T(8,128)S(1)} %copy-done.4, f32[]{:T(128)} %reduce_max.28), kind=kOutput, calls=%fused_computation.10 | convolution fusion | flops 3223322624 | bytes 7340036 | tf_op jit(solution)/shard_map/dot_general | solution.py:14
  212.2 16.2 %fusion.8 = f32[512,512]{1,0:T(8,128)} fusion(f32[4,1024,512]{2,1,0:T(8,128)S(1)} %bitcast.66, f32[4,512]{1,0:T(4,128)S(1)} %fusion.25, f32[1024,512]{0,1:T(8,128)S(1)} %subtract_maximum_fusion), kind=kOutput, calls=%fused_computation.16 | convolution fusion | flops 12886999040 | bytes 11542528 | tf_op jit(solution)/shard_map/ijk,ijr->kr/dot_general | solution.py:38
  228.3 0.0 reduce-scatter.2.cloned.1.call-update
  228.4 4.7 %fusion.81 = (f32[512]{0:T(512)S(1)}, f32[512,512]{0,1:T(8,128)S(1)}) fusion(f32[512,512]{0,1:T(8,128)} %get-tuple-element.7, f32[1024,512]{0,1:T(8,128)S(1)} %subtract_maximum_fusion), kind=kOutput, calls=%fused_computation.98 | convolution fusion | flops 3221749248 | bytes 4196352 | tf_op jit(solution)/shard_map/dot_general | solution.py:39
  233.1 0.6 reduce_max.29
  233.7 0.1 constant_dynamic-slice_fusion
  233.9 0.7 copy.14
  234.6 129.6 %reduce-scatter.2.cloned.1.call-done = f32[16,512]{1,0:T(8,128)} async-done(((f32[512,512]{1,0:T(8,128)}), f32[16,512]{1,0:T(8,128)}) %reduce-scatter.2.cloned.1.call-update) | async-done | bytes 32784 | tf_op jit(solution)/shard_map/reduce_scatter | solution.py:43
  364.2 2.5 fusion.22
  366.6 2.4 fusion.19
  369.1 1.6 fusion.16
  370.7 2.2 fusion.13
  (24 shorter events, 0.1 us)
Async XLA Ops:
  7.2 3.6 copy-start
  7.2 179.5 %all-reduce.3.cloned.1.call-start = ((), (), s32[]{:S(2)}) async-start(), calls=%async_computation.2 | async-start | bytes 6291456 | tf_op jit(solution)/shard_map/psum | solution.py:35
  10.8 3.6 copy-start.1
  15.0 16.6 %copy-start.7 = (f32[4,512]{1,0:T(4,128)S(1)}, f32[4,512]{1,0:T(4,128)}, u32[]{:S(2)}) copy-start(f32[4,512]{1,0:T(4,128)} %param.5) | copy-start | bytes 24580
  38.2 174.0 %copy-start.6 = (f32[4,512]{1,0:T(4,128)}, f32[4,512]{1,0:T(4,128)S(1)}, u32[]{:S(2)}) copy-start(f32[4,512]{1,0:T(4,128)S(1)} %fusion.25) | copy-start | bytes 24580
  45.7 141.0 %copy-start.2 = (f32[512,512]{0,1:T(8,128)S(1)}, f32[512,512]{0,1:T(8,128)}, u32[]{:S(2)}) copy-start(f32[512,512]{0,1:T(8,128)} %copy-done.1) | copy-start | bytes 3145732
  45.7 318.5 %reduce-scatter.2.cloned.1.call-start = ((), (), s32[]{:S(2)}) async-start(), calls=%async_computation.1 | async-start | bytes 1081344 | tf_op jit(solution)/shard_map/reduce_scatter | solution.py:43
  189.7 8.0 %copy-start.3 = (f32[1024,512]{0,1:T(8,128)S(1)}, f32[1024,512]{0,1:T(8,128)}, u32[]{:S(2)}) copy-start(f32[1024,512]{0,1:T(8,128)} %copy.8) | copy-start | bytes 6291460
  189.7 8.0 %copy-start.4 = (f32[512,512]{0,1:T(8,128)S(1)}, f32[512,512]{0,1:T(8,128)}, u32[]{:S(2)}) copy-start(f32[512,512]{0,1:T(8,128)} %get-tuple-element.9) | copy-start | bytes 3145732
  197.7 3.8 copy-start.8
  197.7 14.4 %slice-start = ((s8[8388608]{0:T(1024)(128)(4,1)}), s8[4194304]{0:T(1024)(128)(4,1)S(1)}, s32[]{:S(2)}) async-start(s8[8388608]{0:T(1024)(128)(4,1)} %bitcast.65), calls=%async_computation.3 | async-start | bytes 8388608
  201.5 10.7 %slice-start.1 = ((s8[8388608]{0:T(1024)(128)(4,1)}), s8[4194304]{0:T(1024)(128)(4,1)S(1)}, s32[]{:S(2)}) async-start(s8[8388608]{0:T(1024)(128)(4,1)} %bitcast.65), calls=%async_computation.4 | async-start | bytes 8388608
  364.2 4.9 %copy-start.5 = (f32[16,512]{1,0:T(8,128)S(1)}, f32[16,512]{1,0:T(8,128)}, u32[]{:S(2)}) copy-start(f32[16,512]{1,0:T(8,128)} %reduce-scatter.2.cloned.1.call-done) | copy-start | bytes 98308
Sparse Core Ops, SparseCore 0:
  45.8 140.8 all-reduce.2
  228.5 135.6 reduce-scatter.1
where the time goes:
time: 385 us; the launch traced here: 380 us
  waiting for transfers between devices  269 us (70%)
  matrix products  84.4 us (22%)
  between operations  14.5 us (4%)
  other arithmetic  6.73 us (2%)
  local copies, waits for them, and re-layouts  5.68 us (1%)
    psum x1, waiting for transfers between devices, body(): second_sums = lax.psum(own_term, 'slab')  139 us
    reduce_scatter x1, waiting for transfers between devices, body(): lax.psum_scatter(third_sums, 'slab', scatter_dimension=0, tiled=True)  130 us
    dot_general x12, matrix products, update(): gradient = jnp.dot(extrapolated, gram, precision=highest) - sums  37.6 us
    dot_general x1, matrix products, body(): partial_value = jnp.einsum('ijk,kr->ijr', tensor, third, precision=highest)  16.6 us
    dot_general x1, matrix products, body(): third_sums = jnp.einsum('ijk,ijr->kr', tensor, weighted, precision=highest)  16.2 us
  transfers between devices with their start and end apart: 2, of which 2 were waited for; matrix products, arithmetic and copies ran while one was open for 2% of the time, Pallas kernels for 0%

commit v1 on v0

--- a/solution.py
+++ b/solution.py
@@ -32,7 +32,17 @@
     own_gram = jnp.dot(new_first.T, new_first, precision=highest)
     gram_first = lax.psum(own_gram, "slab")
     own_term = jnp.einsum("ijr,ir->jr", partial_value, new_first, precision=highest)
-    second_sums = lax.psum(own_term, "slab")
+
+    def _fit_limits(a0):
+        bus_axis = "slab"
+        workers = lax.axis_size(bus_axis)
+        step_out = lambda carry_out: [(j, j ^ carry_out) for j in range(workers)]
+        low = a0
+        for nth in range(workers.bit_length() - 1):
+            low = low + lax.ppermute(low, bus_axis, step_out(1 << nth))
+        return low
+
+    second_sums = _fit_limits(own_term)
     whole_second = update(second, second_sums, gram_first * gram_third)
     weighted = whole_second[None, :, :] * new_first[:, None, :]
     third_sums = jnp.einsum("ijk,ijr->kr", tensor, weighted, precision=highest)

time: 385 us -> 598 us (1.55)
  waiting for transfers between devices: 269 us -> 461 us
  starting transfers between devices: 0.08 us -> 9.27 us
  matrix products: 84.4 us -> 90.6 us
    ppermute x0 -> x5, waiting for transfers between devices: none -> 140 us  [_fit_limits(): low = low + lax.ppermute(low, bus_axis, step_out(1 << nth))]
    psum x1, waiting for transfers between devices: 139 us -> 194 us  [body(): gram_first = lax.psum(own_gram, 'slab')]
    ppermute x0 -> x5, starting transfers between devices: none -> 9.19 us  [_fit_limits(): low = low + lax.ppermute(low, bus_axis, step_out(1 << nth))]
  transfers between devices with their start and end apart: 2 -> 7, of which waited for: 2 -> 6; matrix products, arithmetic and copies ran while one was open for 2% -> 2% of each run, Pallas kernels for 0% -> 0%
where the time goes in v1:
time: 598 us; the launch traced here: 593 us
  waiting for transfers between devices  461 us (77%)
  matrix products  90.6 us (15%)
  between operations  14.5 us (2%)
  other arithmetic  11.1 us (2%)
  starting transfers between devices  9.27 us (2%)
  local copies, waits for them, and re-layouts  7 us (1%)
    psum x1, waiting for transfers between devices, body(): gram_first = lax.psum(own_gram, 'slab')  194 us
    ppermute x5, waiting for transfers between devices, _fit_limits(): low = low + lax.ppermute(low, bus_axis, step_out(1 << nth))  140 us
    reduce_scatter x1, waiting for transfers between devices, body(): lax.psum_scatter(third_sums, 'slab', scatter_dimension=0, tiled=True)  127 us
    dot_general x12, matrix products, update(): gradient = jnp.dot(extrapolated, gram, precision=highest) - sums  42.8 us
    dot_general x1, matrix products, body(): partial_value = jnp.einsum('ijk,kr->ijr', tensor, third, precision=highest)  16.6 us
    dot_general x1, matrix products, body(): third_sums = jnp.einsum('ijk,ijr->kr', tensor, weighted, precision=highest)  16.2 us
  transfers between devices with their start and end apart: 7, of which 6 were waited for; matrix products, arithmetic and copies ran while one was open for 2% of the time, Pallas kernels for 0%

profile of v1, /device:TPU:0, one launch (start us, length us, event | category | flops | bytes accessed | tf_op | source)
XLA Modules:
  0.0 593.4 jit_solution(1148539454076565331)
XLA Ops:
  7.2 3.5 fusion.83
  10.8 3.6 fusion.81
  15.0 16.6 %multiply_reduce_fusion.1 = (f32[512,4]{0,1:T(4,128)S(1)}, f32[4,1024,512]{2,1,0:T(8,128)S(1)}) fusion(f32[512,1024]{0,1:T(8,128)S(1)} %bitcast.65, f32[4,1024,512]{2,1,0:T(8,128)} %param.4, f32[512,512]{1,0:T(8,128)} %param.7), kind=kOutput, calls=%fused_computation.1 | convolution fusion | flops 12889094144 | bytes 19931136 | tf_op jit(solution)/shard_map/ijk,kr->ijr/dot_general | solution.py:29
  31.7 1.6 fusion.35
  33.3 1.6 fusion.31
  36.5 1.6 fusion.25
  38.2 2.5 multiply_reduce_fusion
  40.7 3.3 copy.28
  44.6 4.0 collective-permute-done
  48.6 2.0 bitcast_add_fusion
  50.5 2.9 collective-permute-start.1
  53.5 45.9 %collective-permute-done.1 = f32[1024,512]{0,1:T(8,128)S(1)} collective-permute-done((f32[1024,512]{0,1:T(8,128)S(1)}, f32[1024,512]{0,1:T(8,128)S(1)}, u32[]{:S(2)}, u32[]{:S(2)}) %collective-permute-start.1) | collective-permute-done | bytes 2097184 | tf_op jit(solution)/shard_map/ppermute | solution.py:42
  99.9 1.8 collective-permute-start.2
  101.8 45.3 %collective-permute-done.2 = f32[1024,512]{0,1:T(8,128)S(1)} collective-permute-done((f32[1024,512]{0,1:T(8,128)S(1)}, f32[1024,512]{0,1:T(8,128)S(1)}, u32[]{:S(2)}, u32[]{:S(2)}) %collective-permute-start.2) | collective-permute-done | bytes 2097184 | tf_op jit(solution)/shard_map/ppermute | solution.py:42
  149.3 44.7 %collective-permute-done.3 = f32[1024,512]{0,1:T(8,128)S(1)} collective-permute-done((f32[1024,512]{0,1:T(8,128)S(1)}, f32[1024,512]{0,1:T(8,128)S(1)}, u32[]{:S(2)}, u32[]{:S(2)}) %collective-permute-start.3) | collective-permute-done | bytes 2097184 | tf_op jit(solution)/shard_map/ppermute | solution.py:42
  194.0 1.7 add.58
  195.7 2.3 collective-permute-start.4
  198.0 2.1 fusion.84
  200.2 1.9 copy.8
  202.0 193.6 %all-reduce.2.cloned.1.call-done = f32[512,512]{0,1:T(8,128)} async-done(((f32[512,512]{0,1:T(8,128)}), f32[512,512]{0,1:T(8,128)}) %all-reduce.2.cloned.1.call-update) | async-done | bytes 1048592 | tf_op jit(solution)/shard_map/psum | solution.py:33
  395.6 1.8 fusion.80
  398.0 7.2 %fusion.6 = f32[1024,512]{0,1:T(8,128)S(1)} fusion(f32[1024,512]{0,1:T(8,128)} %copy.8, f32[512,512]{0,1:T(8,128)S(1)} %get-tuple-element.7, f32[1024,512]{1,0:T(8,128)S(1)} %copy-done, f32[]{:T(128)} %reduce_max.28, f32[1024,512]{0,1:T(8,128)} %add.58, f32[1024,512]{0,1:T(8,128)} %collective-permute-done.4), kind=kOutput, calls=%fused_computation.9 | convolution fusion | flops 3223846912 | bytes 11534340 | tf_op jit(solution)/shard_map/dot_general | solution.py:14
  405.3 3.7 fusion.40
  408.9 9.8 %multiply_add_fusion = f32[1024,512]{0,1:T(8,128)S(1)} fusion(f32[1024,512]{0,1:T(8,128)S(1)} %fusion.6, f32[512,512]{0,1:T(8,128)S(1)} %get-tuple-element.7, f32[1024,512]{0,1:T(8,128)S(1)} %fusion.40, f32[1024,512]{0,1:T(8,128)S(1)} %copy-done.1, f32[]{:T(128)} %reduce_max.28, f32[1024,512]{0,1:T(8,128)} %add.58, f32[1024,512]{0,1:T(8,128)} %collective-permute-done.4), kind=kOutput, calls=%fused_computation.11 | convolution fusion | flops 3236429824 | bytes 13631492 | tf_op jit(solution)/shard_map/dot_general | solution.py:14
  418.7 6.7 %subtract_maximum_fusion = f32[1024,512]{0,1:T(8,128)S(1)} fusion(f32[1024,512]{0,1:T(8,128)S(1)} %multiply_add_fusion, f32[512,512]{0,1:T(8,128)S(1)} %get-tuple-element.7, f32[]{:T(128)} %reduce_max.28, f32[1024,512]{0,1:T(8,128)} %add.58, f32[1024,512]{0,1:T(8,128)} %collective-permute-done.4), kind=kOutput, calls=%fused_computation.10 | convolution fusion | flops 3223846912 | bytes 9437188 | tf_op jit(solution)/shard_map/dot_general | solution.py:14
  425.5 16.2 %fusion.8 = f32[512,512]{1,0:T(8,128)} fusion(f32[4,1024,512]{2,1,0:T(8,128)S(1)} %bitcast.67, f32[4,512]{1,0:T(4,128)S(1)} %fusion.25, f32[1024,512]{0,1:T(8,128)S(1)} %subtract_maximum_fusion), kind=kOutput, calls=%fused_computation.16 | convolution fusion | flops 12886999040 | bytes 11542528 | tf_op jit(solution)/shard_map/ijk,ijr->kr/dot_general | solution.py:48
  441.7 5.7 fusion.82
  450.0 127.4 %reduce-scatter.2.cloned.1.call-done = f32[16,512]{1,0:T(8,128)} async-done(((f32[512,512]{1,0:T(8,128)}), f32[16,512]{1,0:T(8,128)}) %reduce-scatter.2.cloned.1.call-update) | async-done | bytes 32784 | tf_op jit(solution)/shard_map/reduce_scatter | solution.py:53
  577.3 2.5 fusion.22
  579.8 2.5 fusion.19
  582.3 1.7 fusion.16
  584.0 2.3 fusion.13
  (36 shorter events, 8.8 us)
Async XLA Ops:
  7.2 3.6 copy-start
  7.2 388.4 %all-reduce.2.cloned.1.call-start = ((), (), s32[]{:S(2)}) async-start(), calls=%async_computation.1 | async-start | bytes 2097152 | tf_op jit(solution)/shard_map/psum | solution.py:33
  10.8 3.6 copy-start.3
  15.0 16.6 %copy-start.7 = (f32[4,512]{1,0:T(4,128)S(1)}, f32[4,512]{1,0:T(4,128)}, u32[]{:S(2)}) copy-start(f32[4,512]{1,0:T(4,128)} %param.5) | copy-start | bytes 24580
  38.2 387.3 %copy-start.6 = (f32[4,512]{1,0:T(4,128)}, f32[4,512]{1,0:T(4,128)S(1)}, u32[]{:S(2)}) copy-start(f32[4,512]{1,0:T(4,128)S(1)} %fusion.25) | copy-start | bytes 24580
  44.0 4.6 collective-permute-start
  50.5 48.8 %collective-permute-start.1 = (f32[1024,512]{0,1:T(8,128)S(1)}, f32[1024,512]{0,1:T(8,128)S(1)}, u32[]{:S(2)}, u32[]{:S(2)}) collective-permute-start(f32[1024,512]{0,1:T(8,128)S(1)} %bitcast_add_fusion), channel_id=1, source_target_pairs={{0,2},{1,3},{2,0},{3,1},{4,6},{5,7},{6,4},{7,5},{8,10},{9,11},{10,... | collective-permute-start | bytes 6291464 | tf_op jit(solution)/shard_map/ppermute | solution.py:42
  99.9 47.2 %collective-permute-start.2 = (f32[1024,512]{0,1:T(8,128)S(1)}, f32[1024,512]{0,1:T(8,128)S(1)}, u32[]{:S(2)}, u32[]{:S(2)}) collective-permute-start(f32[1024,512]{0,1:T(8,128)S(1)} %add.56), channel_id=1, source_target_pairs={{0,4},{1,5},{2,6},{3,7},{4,0},{5,1},{6,2},{7,3},{8,12},{9,13},{10,... | collective-permute-start | bytes 6291464 | tf_op jit(solution)/shard_map/ppermute | solution.py:42
  147.7 46.3 %collective-permute-start.3 = (f32[1024,512]{0,1:T(8,128)S(1)}, f32[1024,512]{0,1:T(8,128)S(1)}, u32[]{:S(2)}, u32[]{:S(2)}) collective-permute-start(f32[1024,512]{0,1:T(8,128)S(1)} %add.57), channel_id=1, source_target_pairs={{0,8},{1,9},{2,10},{3,11},{4,12},{5,13},{6,14},{7,15},{8,0},{9,1},... | collective-permute-start | bytes 6291464 | tf_op jit(solution)/shard_map/ppermute | solution.py:42
  195.7 202.3 %collective-permute-start.4 = (f32[1024,512]{0,1:T(8,128)}, f32[1024,512]{0,1:T(8,128)}, u32[]{:S(2)}, u32[]{:S(2)}) collective-permute-start(f32[1024,512]{0,1:T(8,128)} %add.58), channel_id=1, source_target_pairs={{0,16},{1,17},{2,18},{3,19},{4,20},{5,21},{6,22},{7,23},{8,24},{9,... | collective-permute-start | bytes 6291464 | tf_op jit(solution)/shard_map/ppermute | solution.py:42
  200.1 377.2 %reduce-scatter.2.cloned.1.call-start = ((), (), s32[]{:S(2)}) async-start(), calls=%async_computation.2 | async-start | bytes 1081344 | tf_op jit(solution)/shard_map/reduce_scatter | solution.py:53
  398.0 7.2 %copy-start.1 = (f32[1024,512]{0,1:T(8,128)S(1)}, f32[1024,512]{0,1:T(8,128)}, u32[]{:S(2)}) copy-start(f32[1024,512]{0,1:T(8,128)} %copy.8) | copy-start | bytes 6291460
  405.2 20.2 %slice-start = ((s8[8388608]{0:T(1024)(128)(4,1)}), s8[4194304]{0:T(1024)(128)(4,1)S(1)}, s32[]{:S(2)}) async-start(s8[8388608]{0:T(1024)(128)(4,1)} %bitcast.66), calls=%async_computation.3 | async-start | bytes 8388608
  408.9 16.6 %slice-start.1 = ((s8[8388608]{0:T(1024)(128)(4,1)}), s8[4194304]{0:T(1024)(128)(4,1)S(1)}, s32[]{:S(2)}) async-start(s8[8388608]{0:T(1024)(128)(4,1)} %bitcast.66), calls=%async_computation.4 | async-start | bytes 8388608
  425.5 16.2 %copy-start.2 = (f32[1024,512]{0,1:T(8,128)}, f32[1024,512]{0,1:T(8,128)S(1)}, u32[]{:S(2)}) copy-start(f32[1024,512]{0,1:T(8,128)S(1)} %subtract_maximum_fusion) | copy-start | bytes 6291460
  425.5 16.2 %copy-start.4 = (f32[512,512]{0,1:T(8,128)S(1)}, f32[512,512]{0,1:T(8,128)}, u32[]{:S(2)}) copy-start(f32[512,512]{0,1:T(8,128)} %all-reduce.2.cloned.1.call-done) | copy-start | bytes 3145732
  577.3 5.0 copy-start.5
Sparse Core Ops, SparseCore 0:
  200.2 195.3 all-reduce.1
  441.8 135.4 reduce-scatter.1
